TPU v7x, 128 devices: a whole 4x4x4 slice. The times are simulated.
128 devices in a mesh: row: 8 (over y, x_lo), col: 16 (over z, x_hi, core).
Axes of the slice: x: 4 (x_hi: 2, x_lo: 2; x = x_hi * 2 + x_lo), y: 4, z: 4, core: 2. Of those that a mesh axis runs over, the one named last changes fastest.
Arguments:
- context_heads: bfloat16 [16384, 8192], P('row', 'col'), may hold values from -6 to 6
- teacher_proj: bfloat16 [8192, 4096], P('col', 'row'), may hold values from -0.0625 to 0.0625
- teacher_resid: bfloat16 [16384, 4096], P(('row', 'col')), may hold values from -6 to 6
- student_in: bfloat16 [16384, 1024], P(('row', 'col')), may hold values from -24 to 24
- norm_gain: bfloat16 [1024], replicated, may hold values from 0.099609375 to 1.8984375
- qkv_weight: bfloat16 [1024, 3072], replicated
- out_weight: bfloat16 [1024, 1024], replicated, may hold values from -0.1875 to 0.1875
- head_weight: bfloat16 [1024, 4096], replicated, may hold values from -0.1875 to 0.1875
- token_ids: int32 [16384], P(('row', 'col')), may hold values from 0 to 128255, as said below
- doc_ids: int32 [16384], P('row'), may hold values from 0 to 63, never falling along the last dimension, each value on 1 to 1024 neighbouring positions
Outputs:
- target: bfloat16 [16384, 4096], P(('row', 'col'))
- prediction: float32 [16384, 4096], P(('row', 'col'))
- head_grad: float32 [1024, 4096], P(('row', 'col'))
Inputs may be any that keep to these rules, and one draw needn't show every extreme that they name: `token_ids`: ids of 128000 and above are special tokens that the loss skips. `doc_ids`: document numbers never fall along the whole array; a document holds at most half of 2048 positions.
All inputs are finite; a program needn't handle non-finite values.
Results may differ from a plain program's by a relative error of at most 0.012.
The roundings to bfloat16 on the way count: a program that leaves them out, or rounds other values in their place, can miss the bound.
Values may be sent and summed in bfloat16 or wider, within the bound.
No kernel may reach another device: no remote copies, remote signals or barrier semaphores. Data moves between devices by JAX's collectives and lax.ppermute only.
A program may use at most 128 MiB of HBM per device.

v0:
```python
import math

import jax
import jax.numpy as jnp
from jax import lax
from jax.sharding import PartitionSpec as P

HEADS = 16
HEAD_DIM = 64
SPECIAL = 128000


def extended(array, sides, width):
    for axis, dim in sides:
        size, length = (lax.axis_size(axis), array.shape[dim])
        up = [(i, (i + 1) % size) for i in range(size - 1)]
        down = [(j, i) for i, j in up]
        last = lax.slice_in_dim(array, length - width, length, axis=dim)
        initial = lax.slice_in_dim(array, 0, width, axis=dim)
        before = lax.ppermute(last, axis, up)
        after = lax.ppermute(initial, axis, down)
        array = jnp.concatenate([before, array, after], axis=dim)
    return array


def body(
    context_heads,
    teacher_proj,
    teacher_resid,
    student_in,
    norm_gain,
    qkv_weight,
    out_weight,
    head_weight,
    token_ids,
    doc_ids,
):
    tok_rows = student_in.shape[0]
    student_width = student_in.shape[1]
    partial_out = jnp.dot(
        context_heads,
        lax.all_gather(teacher_proj, "row", axis=1, tiled=True),
        preferred_element_type=jnp.float32,
    )
    summed = lax.psum_scatter(
        partial_out.astype(jnp.bfloat16), "col", scatter_dimension=1, tiled=True
    ).astype(jnp.float32)
    teacher_out = lax.all_to_all(
        summed.astype(jnp.bfloat16), "col", split_axis=0, concat_axis=1, tiled=True
    ).astype(summed.dtype)
    target = (teacher_resid.astype(jnp.float32) + teacher_out).astype(jnp.bfloat16)
    student_f = student_in.astype(jnp.float32)
    mean_sq = jnp.mean(student_f * student_f, axis=-1, keepdims=True)
    normed = (student_f * lax.rsqrt(mean_sq + 1e-05) * norm_gain.astype(jnp.float32)).astype(
        jnp.bfloat16
    )
    projected = jnp.dot(normed, qkv_weight, preferred_element_type=jnp.float32).astype(jnp.bfloat16)
    queries = projected[:, :student_width].reshape(tok_rows, HEADS, HEAD_DIM)
    keyvals = projected[:, student_width:]
    widened = extended(keyvals, (("col", 0),), tok_rows)
    keys_all = widened[:, :student_width].reshape(3 * tok_rows, HEADS, HEAD_DIM)
    values_all = widened[:, student_width:].reshape(3 * tok_rows, HEADS, HEAD_DIM)
    col_count = lax.axis_size("col")
    first_pos = lax.axis_index("col") * tok_rows
    query_pos = first_pos + jnp.arange(tok_rows, dtype=jnp.int32)
    key_pos = first_pos - tok_rows + jnp.arange(3 * tok_rows, dtype=jnp.int32)
    filler = jnp.full((tok_rows,), -1, jnp.int32)
    padded_docs = jnp.concatenate([filler, doc_ids, filler])
    query_docs = lax.dynamic_slice_in_dim(doc_ids, first_pos, tok_rows)
    key_docs = lax.dynamic_slice_in_dim(padded_docs, first_pos, 3 * tok_rows)
    allowed = (query_docs[:, None] == key_docs[None, :]) & (
        jnp.abs(query_pos[:, None] - key_pos[None, :]) <= tok_rows
    )
    scores = jnp.einsum("qhd,khd->hqk", queries, keys_all, preferred_element_type=jnp.float32) * (
        1.0 / math.sqrt(HEAD_DIM)
    )
    scores = jnp.where(allowed[None], scores, -jnp.inf)
    row_max = jnp.max(scores, axis=-1, keepdims=True)
    exp_scores = jnp.exp(scores - row_max)
    weights = (exp_scores / jnp.sum(exp_scores, axis=-1, keepdims=True)).astype(jnp.bfloat16)
    attended = jnp.einsum("hqk,khd->qhd", weights, values_all, preferred_element_type=jnp.float32)
    attended = attended.reshape(tok_rows, student_width).astype(jnp.bfloat16)
    hidden = (student_f + jnp.dot(attended, out_weight, preferred_element_type=jnp.float32)).astype(
        jnp.bfloat16
    )
    prediction = jnp.dot(hidden, head_weight, preferred_element_type=jnp.float32)
    loss_mask = (token_ids < SPECIAL).astype(jnp.float32)
    scaled_error = (loss_mask[:, None] * (prediction - target.astype(jnp.float32))).astype(
        jnp.bfloat16
    )
    seq_len = tok_rows * col_count
    product = lax.dot_general(
        hidden, scaled_error, (((0,), (0,)), ((), ())), preferred_element_type=jnp.float32
    )
    head_grad = lax.psum_scatter(
        product * (1.0 / seq_len), ("row", "col"), scatter_dimension=0, tiled=True
    )
    return (target, prediction, head_grad)


def solution(mesh):
    return jax.shard_map(
        body,
        mesh=mesh,
        in_specs=(
            P("row", "col"),
            P("col", "row"),
            P(("row", "col"), None),
            P(("row", "col"), None),
            P(),
            P(),
            P(),
            P(),
            P(("row", "col")),
            P("row"),
        ),
        out_specs=(P(("row", "col"), None), P(("row", "col"), None), P(("row", "col"), None)),
        check_vma=False,
    )
```

profile of v0, /device:TPU:0, one launch (start us, length us, event | category | flops | bytes accessed | tf_op | source)
XLA Modules:
  0.0 979.3 jit_solution(2185386041618945290)
XLA Ops:
  7.2 0.0 copy-start
  7.2 0.0 all-gather.2.cloned.1.call-start
  7.2 0.7 all-gather.2.cloned.1.call-update
  7.9 0.0 reduce-scatter.3.cloned.1.call-start
  8.0 95.0 %all-gather.2.cloned.1.call-done = bf16[512,4096]{1,0:T(8,128)(2,1)} async-done(((bf16[512,512]{1,0:T(8,128)(2,1)}), bf16[512,4096]{1,0:T(8,128)(2,1)}) %all-gather.2.cloned.1.call-update) | async-done | bytes 4194320 | tf_op jit(solution)/shard_map/all_gather | solution.py:42
  102.9 0.0 copy-done
  102.9 13.9 %convolution_convert_fusion = bf16[2048,4096]{1,0:T(8,128)(2,1)} fusion(bf16[2048,512]{1,0:T(8,128)(2,1)S(1)} %copy-done, bf16[512,4096]{1,0:T(8,128)(2,1)} %all-gather.2.cloned.1.call-done), kind=kOutput, calls=%fused_computation.1 | convolution fusion | flops 8598323200 | bytes 23068672 | tf_op jit(solution)/shard_map/dot_general | solution.py:40
  116.8 0.0 reduce-scatter.3.cloned.1.call-update
  116.8 0.7 copy-done.8
  117.5 0.3 copy-done.4
  117.8 0.1 fusion.9
  117.9 0.0 copy-start.9
  117.9 3.9 convolution_convert_fusion.1
  121.8 1.3 collective-permute-start.1
  123.1 3.8 collective-permute-start
  127.0 0.2 copy.19
  127.2 0.0 copy-done.7
  127.2 0.1 dynamic_slice.6
  127.3 0.1 fusion.19
  127.4 0.0 copy-done.9
  127.4 0.1 fusion.17
  127.5 0.0 collective-permute-done.1
  127.5 0.7 collective-permute-done
  128.2 1.3 pad_maximum_fusion
  129.5 1.0 fusion.22
  130.5 1.6 copy.18
  132.1 0.4 copy.20
  132.4 2.8 fusion.23
  135.3 128.6 %reduce-scatter.3.cloned.1.call-done = bf16[2048,256]{1,0:T(8,128)(2,1)} async-done(((bf16[2048,4096]{1,0:T(8,128)(2,1)}), bf16[2048,256]{1,0:T(8,128)(2,1)}) %reduce-scatter.3.cloned.1.call-update) | async-done | bytes 1048592 | tf_op jit(solution)/shard_map/reduce_scatter | solution.py:45
  263.9 3.7 all-to-all-start
  267.6 0.0 reduce-scatter.5.cloned.1.call-start
  267.6 0.0 copy-start.5
  267.7 2.9 fusion.6
  270.6 0.0 copy-done.5
  270.6 0.5 fusion.7
  271.1 4.6 fusion.24
  275.7 0.0 copy-start.2
  275.7 9.8 %all-to-all-done = bf16[16,128,256]{2,1,0:T(8,128)(2,1)S(1)} async-done(((bf16[16,128,256]{2,1,0:T(8,128)(2,1)}), bf16[16,128,256]{2,1,0:T(8,128)(2,1)S(1)}, u32[]{:S(2)}, u32[]{:S(2)}) %all-to-all-start) | async-done | bytes 1048608 | tf_op jit(solution)/shard_map/all_to_all | solution.py:48
  285.6 0.2 convert_bitcast_fusion
  285.8 0.2 copy.21
  286.0 0.8 copy-done.6
  286.8 0.2 add_convert_fusion
  287.0 0.0 copy-done.2
  287.0 0.0 copy-start.3
  287.0 8.2 convolution_multiply_fusion
  295.2 0.0 reduce-scatter.5.cloned.1.call-update
  295.2 0.0 copy-start.1
  295.2 677.5 %reduce-scatter.5.cloned.1.call-done = f32[8,4096]{1,0:T(8,128)} async-done(((f32[1024,4096]{1,0:T(8,128)}), f32[8,4096]{1,0:T(8,128)}) %reduce-scatter.5.cloned.1.call-update) | async-done | bytes 131088 | tf_op jit(solution)/shard_map/reduce_scatter | solution.py:95
  (13 shorter events, 0.1 us)
Async XLA Ops:
  7.2 95.8 %copy-start = (bf16[2048,512]{1,0:T(8,128)(2,1)S(1)}, bf16[2048,512]{1,0:T(8,128)(2,1)}, u32[]{:S(2)}) copy-start(bf16[2048,512]{1,0:T(8,128)(2,1)} %param.10) | copy-start | bytes 6291460
  7.2 95.8 %all-gather.2.cloned.1.call-start = ((), (), s32[]{:S(2)}) async-start(), calls=%async_computation.3 | async-start | bytes 4718592 | tf_op jit(solution)/shard_map/all_gather | solution.py:42
  7.9 256.0 %reduce-scatter.3.cloned.1.call-start = ((), (), s32[]{:S(2)}) async-start(), calls=%async_computation.4 | async-start | bytes 17825792 | tf_op jit(solution)/shard_map/reduce_scatter | solution.py:45
  116.8 0.7 copy-start.8
  116.8 1.0 copy-start.4
  117.9 9.3 copy-start.7
  117.9 9.4 copy-start.9
  121.8 5.7 collective-permute-start.1
  123.1 5.1 collective-permute-start
  263.9 21.6 %all-to-all-start = ((bf16[16,128,256]{2,1,0:T(8,128)(2,1)}), bf16[16,128,256]{2,1,0:T(8,128)(2,1)S(1)}, u32[]{:S(2)}, u32[]{:S(2)}) async-start(bf16[16,128,256]{2,1,0:T(8,128)(2,1)} %bitcast.25), calls=%async_computation.1 | async-start | bytes 2097152 | tf_op jit(solution)/shard_map/all_to_all | solution.py:48
  267.6 705.1 %reduce-scatter.5.cloned.1.call-start = ((), (), s32[]{:S(2)}) async-start(), calls=%async_computation.5 | async-start | bytes 16908288 | tf_op jit(solution)/shard_map/reduce_scatter | solution.py:95
  267.6 2.9 copy-start.5
  275.7 11.3 %copy-start.2 = (f32[128,4096]{1,0:T(8,128)}, f32[128,4096]{1,0:T(8,128)S(1)}, u32[]{:S(2)}) copy-start(f32[128,4096]{1,0:T(8,128)S(1)} %fusion.24) | copy-start | bytes 6291460
  285.6 1.2 copy-start.6
  287.0 8.2 copy-start.3
  295.2 677.5 %copy-start.1 = (bf16[2048,512]{1,0:T(8,128)(2,1)S(1)}, bf16[2048,512]{1,0:T(8,128)(2,1)}, u32[]{:S(2)}) copy-start(bf16[2048,512]{1,0:T(8,128)(2,1)} %param.10) | copy-start | bytes 6291460
Sparse Core Ops, SparseCore 0:
  9.6 93.2 all-gather.1
  117.0 146.9 reduce-scatter.2
  295.4 677.3 reduce-scatter.4
where the time goes:
time: 980 us; the launch traced here: 979 us
  waiting for transfers between devices  912 us (93%)
  matrix products  36.8 us (4%)
  between operations  14 us (1%)
    reduce_scatter x1, waiting for transfers between devices, body(): lax.psum_scatter(product * (1.0 / seq_len), ('row', 'col'), scatter_dimen...  677 us
    reduce_scatter x1, waiting for transfers between devices, body(): lax.psum_scatter(partial_out.astype(jnp.bfloat16), 'col', scatter_dimensi...  129 us
    all_gather x1, waiting for transfers between devices, body(): lax.all_gather(teacher_proj, 'row', axis=1, tiled=True)  95 us
  transfers between devices with their start and end apart: 6, of which 5 were waited for; matrix products, arithmetic and copies ran while one was open for 2% of the time, Pallas kernels for 0%

commit v1 on v0

v1 whole, which is shorter than its diff:
```python
import math

import jax
import jax.numpy as jnp
from jax import lax
from jax.experimental import pallas as pl
from jax.experimental.pallas import tpu as pltpu
from jax.sharding import Mesh
from jax.sharding import PartitionSpec as P

HEADS = 16
HEAD_DIM = 64
SPECIAL = 128000

AXES = ("y", "xl", "z", "xh", "core")
SIZES = (4, 2, 4, 2, 2)
COL = ("z", "xh", "core")


def exchange(blocks, axes):
    return lax.all_to_all(blocks, axes, 0, 0, tiled=True)


def spread(array, axes):
    size = math.prod(lax.axis_size(axis) for axis in axes)
    return exchange(jnp.broadcast_to(array[None], (size, *array.shape)), axes)


def partial_kernel(core_ref, a_ref, own_ref, other_ref, out_ref):
    core = core_ref[0]
    total = None
    for ref, side in ((own_ref, core), (other_ref, 1 - core)):
        for half in range(2):
            term = jnp.dot(
                a_ref[half, side], ref[0, 0, half], preferred_element_type=jnp.float32
            ).astype(jnp.bfloat16)
            term = term.astype(jnp.float32)
            total = term if total is None else total + term
    out_ref[0] = total.astype(jnp.bfloat16)


def teacher_partials(heads, own, other):
    _, _, tokens, depth = heads.shape
    ysize, xsize, _, _, width = own.shape
    core = lax.axis_index("core").astype(jnp.int32).reshape(1)
    weight_spec = pl.BlockSpec(
        (1, 1, 2, depth, width), lambda i, _: (i // xsize, i % xsize, 0, 0, 0)
    )
    return pl.pallas_call(
        partial_kernel,
        out_shape=jax.ShapeDtypeStruct((ysize * xsize, tokens, width), jnp.bfloat16),
        grid_spec=pltpu.PrefetchScalarGridSpec(
            num_scalar_prefetch=1,
            grid=(ysize * xsize,),
            in_specs=[
                pl.BlockSpec(heads.shape, lambda i, _: (0, 0, 0, 0)),
                weight_spec,
                weight_spec,
            ],
            out_specs=pl.BlockSpec((1, tokens, width), lambda i, _: (i, 0, 0)),
        ),
        compiler_params=pltpu.CompilerParams(vmem_limit_bytes=48 * 1024 * 1024),
        name="teacher_partials",
    )(core, heads, own, other)


def neighbours(array):
    size = math.prod(lax.axis_size(axis) for axis in COL)
    up = [(i, i + 1) for i in range(size - 1)]
    down = [(i + 1, i) for i in range(size - 1)]
    return lax.ppermute(array, COL, up), lax.ppermute(array, COL, down)


def student_hidden(student_in, norm_gain, qkv_weight, out_weight, doc_ids):
    tok_rows, student_width = student_in.shape
    student_f = student_in.astype(jnp.float32)
    mean_sq = jnp.mean(student_f * student_f, axis=-1, keepdims=True)
    normed = (student_f * lax.rsqrt(mean_sq + 1e-05) * norm_gain.astype(jnp.float32)).astype(
        jnp.bfloat16
    )
    projected = jnp.dot(normed, qkv_weight, preferred_element_type=jnp.float32).astype(jnp.bfloat16)
    queries = projected[:, :student_width].reshape(tok_rows, HEADS, HEAD_DIM)
    keyvals = projected[:, student_width:]
    before, after = neighbours(keyvals)
    widened = jnp.concatenate([before, keyvals, after], axis=0)
    keys_all = widened[:, :student_width].reshape(3 * tok_rows, HEADS, HEAD_DIM)
    values_all = widened[:, student_width:].reshape(3 * tok_rows, HEADS, HEAD_DIM)
    first_pos = lax.axis_index(COL) * tok_rows
    query_pos = first_pos + jnp.arange(tok_rows, dtype=jnp.int32)
    key_pos = first_pos - tok_rows + jnp.arange(3 * tok_rows, dtype=jnp.int32)
    filler = jnp.full((tok_rows,), -1, jnp.int32)
    padded_docs = jnp.concatenate([filler, doc_ids, filler])
    query_docs = lax.dynamic_slice_in_dim(doc_ids, first_pos, tok_rows)
    key_docs = lax.dynamic_slice_in_dim(padded_docs, first_pos, 3 * tok_rows)
    allowed = (query_docs[:, None] == key_docs[None, :]) & (
        jnp.abs(query_pos[:, None] - key_pos[None, :]) <= tok_rows
    )
    scores = jnp.einsum("qhd,khd->hqk", queries, keys_all, preferred_element_type=jnp.float32) * (
        1.0 / math.sqrt(HEAD_DIM)
    )
    scores = jnp.where(allowed[None], scores, -jnp.inf)
    row_max = jnp.max(scores, axis=-1, keepdims=True)
    exp_scores = jnp.exp(scores - row_max)
    weights = (exp_scores / jnp.sum(exp_scores, axis=-1, keepdims=True)).astype(jnp.bfloat16)
    attended = jnp.einsum("hqk,khd->qhd", weights, values_all, preferred_element_type=jnp.float32)
    attended = attended.reshape(tok_rows, student_width).astype(jnp.bfloat16)
    return (student_f + jnp.dot(attended, out_weight, preferred_element_type=jnp.float32)).astype(
        jnp.bfloat16
    )


def body(
    context_heads,
    teacher_proj,
    teacher_resid,
    student_in,
    norm_gain,
    qkv_weight,
    out_weight,
    head_weight,
    token_ids,
    doc_ids,
):
    tok_rows, student_width = student_in.shape
    row_tokens, depth = context_heads.shape
    out_width = teacher_resid.shape[1]
    width = teacher_proj.shape[1] // 2
    ysize, xlsize, zsize = (lax.axis_size(axis) for axis in ("y", "xl", "z"))
    colsize = 4 * zsize

    halves = jnp.swapaxes(teacher_proj.reshape(depth, 2, width), 0, 1)
    along_x = exchange(jnp.concatenate([halves] * xlsize), ("xl", "xh"))
    own = spread(along_x, ("y",)).reshape(ysize, xlsize, 2, depth, width)
    other = lax.ppermute(own, "core", [(0, 1), (1, 0)])

    heads = exchange(
        jnp.concatenate([context_heads.reshape(2, row_tokens // 2, depth)] * 2), ("xh", "core")
    ).reshape(2, 2, row_tokens // 2, depth)
    partials = teacher_partials(heads, own, other)
    received = exchange(partials, ("z", "core"))
    summed = jnp.sum(
        received.reshape(zsize, row_tokens, width).astype(jnp.float32), axis=0
    )

    by_owner = teacher_resid.reshape(tok_rows, zsize, 2, 2, width).transpose(1, 3, 2, 0, 4)
    resid_cols = exchange(by_owner.reshape(colsize, tok_rows, width), COL)
    target_cols = (
        resid_cols.reshape(row_tokens, width).astype(jnp.float32) + summed
    ).astype(jnp.bfloat16)
    target = exchange(target_cols.reshape(colsize, tok_rows, width), COL)
    target = target.reshape(zsize, 2, 2, tok_rows, width).transpose(3, 0, 2, 1, 4)
    target = target.reshape(tok_rows, out_width)

    hidden = student_hidden(student_in, norm_gain, qkv_weight, out_weight, doc_ids)
    prediction = jnp.dot(hidden, head_weight, preferred_element_type=jnp.float32)

    kept = jnp.where((token_ids < SPECIAL)[:, None], hidden, jnp.zeros_like(hidden))
    kept_all = spread(spread(spread(kept, ("xh",)), ("z",)), ("core",))
    kept_all = kept_all.reshape(2, zsize, 2, tok_rows, student_width).transpose(1, 2, 0, 3, 4)
    kept_all = kept_all.reshape(row_tokens, student_width)
    z, xh, core = (lax.axis_index(axis) for axis in COL)
    block = z * 4 + core * 2 + xh
    weight_cols = lax.dynamic_slice_in_dim(head_weight, block * width, width, axis=1)
    predicted = jnp.dot(kept_all, weight_cols, preferred_element_type=jnp.float32)
    error = (predicted - target_cols.astype(jnp.float32)).astype(jnp.bfloat16)
    product = lax.dot_general(
        kept_all, error, (((0,), (0,)), ((), ())), preferred_element_type=jnp.float32
    )
    everyone = math.prod(SIZES)
    pieces = exchange(product.reshape(everyone, student_width // everyone, width), AXES)
    grad = jnp.sum(
        pieces.reshape(ysize * xlsize, zsize, 2, 2, student_width // everyone, width), axis=0
    ) * (1.0 / row_tokens)
    head_grad = grad.transpose(3, 0, 2, 1, 4).reshape(student_width // everyone, out_width)
    return (target, prediction, head_grad)


def solution(mesh):
    fine = Mesh(mesh.devices.reshape(SIZES), AXES)
    row, col, whole = (("y", "xl"), COL, AXES)
    return jax.shard_map(
        body,
        mesh=fine,
        in_specs=(
            P(row, col),
            P(col, row),
            P(whole, None),
            P(whole, None),
            P(),
            P(),
            P(),
            P(),
            P(whole),
            P(row),
        ),
        out_specs=(P(whole, None), P(whole, None), P(whole, None)),
        check_vma=False,
    )
```

time: 980 us -> 355 us (0.36)
  waiting for transfers between devices: 912 us -> 96.5 us
  blocking collectives: 0 us -> 126 us
  starting transfers between devices: 8.9 us -> 42.4 us
  local copies, waits for them, and re-layouts: 5.23 us -> 33.9 us
  between operations: 14 us -> 0.95 us
  Pallas kernels: 0 us -> 12.8 us
  other arithmetic: 2.09 us -> 13.7 us
  matrix products: 36.8 us -> 26.4 us
    reduce_scatter x2 -> x0, waiting for transfers between devices: 806 us -> none  [the longest x1 677 us: body(): lax.psum_scatter(product * (1.0 / seq_len), ('row', 'col'), scatter_dimen...]
    all_to_all x0 -> x3, blocking collectives: none -> 126 us  [exchange(): return lax.all_to_all(blocks, axes, 0, 0, tiled=True)]
    all_gather x1 -> x0, waiting for transfers between devices: 95 us -> none  [body(): lax.all_gather(teacher_proj, 'row', axis=1, tiled=True)]
    all_to_all x1 -> x7, waiting for transfers between devices: 9.81 us -> 96.5 us  [exchange(): return lax.all_to_all(blocks, axes, 0, 0, tiled=True)]
    all_to_all x1 -> x7, starting transfers between devices: 3.65 us -> 37.2 us  [exchange(): return lax.all_to_all(blocks, axes, 0, 0, tiled=True)]
    dot_general x5 -> x4, matrix products: 29.3 us -> 16.3 us  [the longest x1 9.02 us: body(): lax.dot_general(kept_all, error, (((0,), (0,)), ((), ())), preferred_elem...]
    pallas_call x0 -> x1, Pallas kernels: none -> 12.8 us  [teacher_partials(): pl.pallas_call(partial_kernel, out_shape=jax.ShapeDtypeStruct((ysize * xs...]
  transfers between devices with their start and end apart: 6 -> 10, of which waited for: 5 -> 6; matrix products, arithmetic and copies ran while one was open for 2% -> 14% of each run, Pallas kernels for 0% -> 4%
where the time goes in v1:
time: 355 us; the launch traced here: 353 us
  blocking collectives  126 us (35%)
  waiting for transfers between devices  96.5 us (27%)
  starting transfers between devices  42.4 us (12%)
  local copies, waits for them, and re-layouts  33.9 us (10%)
  matrix products  26.4 us (7%)
  other arithmetic  13.7 us (4%)
  Pallas kernels  12.8 us (4%)
    all_to_all x3, blocking collectives, exchange(): return lax.all_to_all(blocks, axes, 0, 0, tiled=True)  126 us
    all_to_all x7, waiting for transfers between devices, exchange(): return lax.all_to_all(blocks, axes, 0, 0, tiled=True)  96.5 us
    all_to_all x7, starting transfers between devices, exchange(): return lax.all_to_all(blocks, axes, 0, 0, tiled=True)  37.2 us
    pallas_call x1, Pallas kernels, teacher_partials(): pl.pallas_call(partial_kernel, out_shape=jax.ShapeDtypeStruct((ysize * xs...  12.8 us
    dot_general x1, matrix products, body(): lax.dot_general(kept_all, error, (((0,), (0,)), ((), ())), preferred_elem...  9.02 us
  transfers between devices with their start and end apart: 10, of which 6 were waited for; matrix products, arithmetic and copies ran while one was open for 14% of the time, Pallas kernels for 4%

profile of v1, /device:TPU:0, one launch (start us, length us, event | category | flops | bytes accessed | tf_op | source)
XLA Modules:
  0.0 353.0 jit_solution(11088815544569605388)
XLA Ops:
  0.6 0.8 convert_element_type.59
  1.5 1.1 fusion.13
  2.6 4.0 %convolution_convert_fusion = bf16[128,3072]{1,0:T(8,128)(2,1)S(1)} fusion(bf16[1024,3072]{1,0:T(8,128)(2,1)} %param.15, bf16[128,1024]{1,0:T(8,128)(2,1)} %param.13, f32[1024]{0:T(1024)S(1)} %convert_element_type.59, f32[128]{0:T(128)S(1)} %add_rsqrt_fusion), kind=kOutput, calls=%fused_computation.5 | convolution fusion | flops 806223872 | bytes 7344640 | tf_op jit(solution)/shard_map/dot_general | solution.py:81
  6.6 1.3 collective-permute-start.2
  7.9 3.8 %collective-permute-start.1 = (bf16[128,2048]{1,0:T(8,128)(2,1)S(1)}, bf16[128,2048]{1,0:T(8,128)(2,1)}, u32[]{:S(2)}, u32[]{:S(2)}) collective-permute-start(bf16[128,2048]{1,0:T(8,128)(2,1)S(1)} %slice.16), channel_id=1, source_target_pairs={{0,1},{1,2},{2,3},{3,4},{4,5},{5,6},{6,7},{7,8},{8,9},{9,10},{10,1... | collective-permute-start | bytes 1572872 | tf_op jit(solution)/shard_map/ppermute | solution.py:71
  11.7 0.7 slice.18
  12.5 1.8 copy.47
  14.6 1.3 pad_maximum_fusion.1
  15.9 1.0 fusion.30
  16.9 2.3 copy.46
  19.2 1.2 copy.48
  20.4 4.0 %fusion.31 = (f32[16,128]{1,0:T(8,128)S(1)}, f32[16,128,384]{2,1,0:T(8,128)}) fusion(pred[128,384]{1,0:T(8,128)(4,1)S(1)} %fusion.23, bf16[128,16,64]{0,2,1:T(8,128)(2,1)S(1)} %bitcast.69, bf16[384,16,64]{0,2,1:T(8,128)(2,1)} %bitcast.68), kind=kOutput, calls=%fused_computation.51 | convolution fusion | flops 103809408 | bytes 4251648 | tf_op jit(solution)/shard_map/sub | solution.py:103
  24.4 2.8 fusion.11
  27.7 0.9 broadcast_in_dim.38
  28.6 10.4 %all-to-all-start.6 = ((bf16[2,128,1024]{2,1,0:T(8,128)(2,1)}), bf16[2,128,1024]{2,1,0:T(8,128)(2,1)S(1)}, u32[]{:S(2)}, u32[]{:S(2)}) async-start(bf16[2,128,1024]{2,1,0:T(8,128)(2,1)} %broadcast_in_dim.38), calls=%async_computation.6 | async-start | bytes 1048576 | tf_op jit(solution)/shard_map/all_to_all | solution.py:21
  39.3 0.5 copy.44
  39.8 9.2 %all-to-all-done.6 = bf16[2,128,1024]{2,1,0:T(8,128)(2,1)S(1)} async-done(((bf16[2,128,1024]{2,1,0:T(8,128)(2,1)}), bf16[2,128,1024]{2,1,0:T(8,128)(2,1)S(1)}, u32[]{:S(2)}, u32[]{:S(2)}) %all-to-all-start.6) | async-done | bytes 524320 | tf_op jit(solution)/shard_map/all_to_all | solution.py:21
  49.1 18.3 %all_to_all.50 = bf16[4,512,256]{2,1,0:T(8,128)(2,1)S(1)} all-to-all(bf16[4,512,256]{2,1,0:T(8,128)(2,1)S(1)} %copy.44), channel_id=1, replica_groups=mesh['y'=4,'xl'=2,'z'=4,'xh'=2,'core'=2] {'xl','xh'}, dimensions={0} | all-to-all | bytes 2097152 | tf_op jit(solution)/shard_map/all_to_all | solution.py:21
  67.8 52.8 %all_to_all.51 = bf16[4,4,512,256]{3,2,1,0:T(8,128)(2,1)} all-to-all(bf16[4,4,512,256]{3,2,1,0:T(8,128)(2,1)S(1)} %broadcast_in_dim.32), channel_id=1, replica_groups=mesh['y'=4,'xl'=2,'z'=4,'xh'=2,'core'=2] {'y'}, dimensions={0} | all-to-all | bytes 8388608 | tf_op jit(solution)/shard_map/all_to_all | solution.py:21
  120.6 1.6 broadcast_in_dim.39
  122.2 3.6 %all-to-all-start.7 = ((bf16[4,2,128,1024]{3,2,1,0:T(8,128)(2,1)}), bf16[4,2,128,1024]{3,2,1,0:T(8,128)(2,1)S(1)}, u32[]{:S(2)}, u32[]{:S(2)}) async-start(bf16[4,2,128,1024]{3,2,1,0:T(8,128)(2,1)} %broadcast_in_dim.39), calls=%async_computation.7 | async-start | bytes 4194304 | tf_op jit(solution)/shard_map/all_to_all | solution.py:21
  125.9 4.6 %pad_maximum_fusion = bf16[4,1024,512]{2,1,0:T(8,128)(2,1)} fusion(bf16[2,1024,512]{2,1,0:T(8,128)(2,1)} %bitcast.65), kind=kLoop, calls=%fused_computation.2 | loop fusion | flops 2097152 | bytes 6291456 | tf_op jit(solution)/shard_map/concatenate | solution.py:137
  130.4 20.1 %all-to-all-done.7 = bf16[4,2,128,1024]{3,2,1,0:T(8,128)(2,1)S(1)} async-done(((bf16[4,2,128,1024]{3,2,1,0:T(8,128)(2,1)}), bf16[4,2,128,1024]{3,2,1,0:T(8,128)(2,1)S(1)}, u32[]{:S(2)}, u32[]{:S(2)}) %all-to-all-start.7) | async-done | bytes 2097184 | tf_op jit(solution)/shard_map/all_to_all | solution.py:21
  150.6 55.3 %all_to_all.52 = bf16[4,1024,512]{2,1,0:T(8,128)(2,1)} all-to-all(bf16[4,1024,512]{2,1,0:T(8,128)(2,1)} %pad_maximum_fusion), channel_id=1, replica_groups=mesh['y'=4,'xl'=2,'z'=4,'xh'=2,'core'=2] {'xh','core'}, dimensions={0} | all-to-all | bytes 8388608 | tf_op jit(solution)/shard_map/all_to_all | solution.py:21
  205.9 2.5 broadcast_in_dim.40
  208.4 5.6 %all-to-all-start.8 = ((bf16[2,4,2,128,1024]{4,3,2,1,0:T(8,128)(2,1)}), bf16[2,4,2,128,1024]{4,3,2,1,0:T(8,128)(2,1)}, u32[]{:S(2)}, u32[]{:S(2)}) async-start(bf16[2,4,2,128,1024]{4,3,2,1,0:T(8,128)(2,1)} %broadcast_in_dim.40), calls=%async_computation.8 | async-start | bytes 8388608 | tf_op jit(solution)/shard_map/all_to_all | solution.py:21
  214.1 12.8 %teacher_partials.1 = bf16[8,1024,256]{2,1,0:T(8,128)(2,1)S(1)} custom-call(s32[1]{0:T(128)} %bitcast.3.core_ref, bf16[2,2,1024,512]{3,2,1,0:T(8,128)(2,1)} %bitcast.59, bf16[4,2,2,512,256]{4,3,2,1,0:T(8,128)(2,1)} %bitcast.58, bf16[4,2,2,512,256]{4,3,2,1,0:T(8,128)(2,1)} %collective-permute-done.other_ref), custom_call_target="tpu_custom_call" | custom-call | tf_op jit(solution)/shard_map/teacher_partials/pallas_call | solution.py:49
  226.9 2.0 copy-done.2
  228.9 4.7 %all-to-all-start.4 = ((bf16[8,1024,256]{2,1,0:T(8,128)(2,1)}), bf16[8,1024,256]{2,1,0:T(8,128)(2,1)}, u32[]{:S(2)}, u32[]{:S(2)}) async-start(bf16[8,1024,256]{2,1,0:T(8,128)(2,1)} %copy-done.2), calls=%async_computation.4 | async-start | bytes 8388608 | tf_op jit(solution)/shard_map/all_to_all | solution.py:21
  233.6 0.7 copy.41
  234.3 1.3 copy.42
  235.6 47.6 %all-to-all-done.4 = bf16[8,1024,256]{2,1,0:T(8,128)(2,1)} async-done(((bf16[8,1024,256]{2,1,0:T(8,128)(2,1)}), bf16[8,1024,256]{2,1,0:T(8,128)(2,1)}, u32[]{:S(2)}, u32[]{:S(2)}) %all-to-all-start.4) | async-done | bytes 4194336 | tf_op jit(solution)/shard_map/all_to_all | solution.py:21
  283.2 3.7 %all-to-all-start = ((bf16[16,128,256]{2,1,0:T(8,128)(2,1)}), bf16[16,128,256]{2,1,0:T(8,128)(2,1)S(1)}, u32[]{:S(2)}, u32[]{:S(2)}) async-start(bf16[16,128,256]{2,1,0:T(8,128)(2,1)} %bitcast.2), calls=%async_computation | async-start | bytes 2097152 | tf_op jit(solution)/shard_map/all_to_all | solution.py:21
  286.9 4.8 %copy.49 = bf16[2,4,2,128,1024]{4,3,0,2,1:T(8,128)(2,1)} copy(bf16[2,4,2,128,1024]{4,3,2,1,0:T(8,128)(2,1)} %all-to-all-done.8) | data formatting | bytes 8388608 | tf_op jit(solution)/shard_map/all_to_all | solution.py:21
  291.7 6.6 %copy.50 = bf16[1024,2048]{1,0:T(8,128)(2,1)} copy(bf16[1024,2048]{0,1:T(8,128)(2,1)} %bitcast.60) | data formatting | bytes 8388608 | tf_op jit(solution)/shard_map/dot_general | solution.py:166
  298.2 3.0 convert_reduce_fusion
  301.2 3.6 %all-to-all-done = bf16[16,128,256]{2,1,0:T(8,128)(2,1)S(1)} async-done(((bf16[16,128,256]{2,1,0:T(8,128)(2,1)}), bf16[16,128,256]{2,1,0:T(8,128)(2,1)S(1)}, u32[]{:S(2)}, u32[]{:S(2)}) %all-to-all-start) | async-done | bytes 1048608 | tf_op jit(solution)/shard_map/all_to_all | solution.py:21
  304.9 1.3 add_convert_fusion
  306.1 4.5 %all-to-all-start.5 = ((bf16[16,128,256]{2,1,0:T(8,128)(2,1)}), bf16[16,128,256]{2,1,0:T(8,128)(2,1)}, u32[]{:S(2)}, u32[]{:S(2)}) async-start(bf16[16,128,256]{2,1,0:T(8,128)(2,1)} %add_convert_fusion), calls=%async_computation.5 | async-start | bytes 2097152 | tf_op jit(solution)/shard_map/all_to_all | solution.py:21
  310.7 1.2 fusion.6
  311.9 9.0 %fusion.1 = f32[128,8,256]{2,1,0:T(8,128)} fusion(bf16[1024,2048]{1,0:T(8,128)(2,1)} %copy.50, bf16[2048,1024]{1,0:T(8,128)(2,1)} %bitcast.61, bf16[2048,256]{1,0:T(8,128)(2,1)} %fusion.6, bf16[1024,4096]{1,0:T(8,128)(2,1)} %param.17, s32[]{:T(128)S(6)} %select_n.21), kind=kOutput, calls=%fused_computation.3 | convolution fusion | flops 2149056512 | bytes 11010052 | tf_op jit(solution)/shard_map/dot_general | solution.py:166
  320.9 7.6 %all-to-all-done.5 = bf16[16,128,256]{2,1,0:T(8,128)(2,1)} async-done(((bf16[16,128,256]{2,1,0:T(8,128)(2,1)}), bf16[16,128,256]{2,1,0:T(8,128)(2,1)}, u32[]{:S(2)}, u32[]{:S(2)}) %all-to-all-start.5) | async-done | bytes 1048608 | tf_op jit(solution)/shard_map/all_to_all | solution.py:21
  328.5 4.6 %all-to-all-start.9 = ((f32[128,8,256]{2,1,0:T(8,128)}), f32[128,8,256]{2,1,0:T(8,128)S(1)}, u32[]{:S(2)}, u32[]{:S(2)}) async-start(f32[128,8,256]{2,1,0:T(8,128)} %fusion.1), calls=%async_computation.9 | async-start | bytes 2097152 | tf_op jit(solution)/shard_map/all_to_all | solution.py:21
  333.1 6.1 %fusion.32 = f32[128,4096]{1,0:T(8,128)} fusion(bf16[128,1024]{1,0:T(8,128)(2,1)S(1)} %get-tuple-element.17, bf16[1024,4096]{1,0:T(8,128)(2,1)} %param.17), kind=kOutput, calls=%fused_computation.52 | convolution fusion | flops 1073741824 | bytes 10747904 | tf_op jit(solution)/shard_map/dot_general | solution.py:155
  339.3 2.3 copy.45
  341.5 2.3 copy.52
  343.8 8.3 %all-to-all-done.9 = f32[128,8,256]{2,1,0:T(8,128)S(1)} async-done(((f32[128,8,256]{2,1,0:T(8,128)}), f32[128,8,256]{2,1,0:T(8,128)S(1)}, u32[]{:S(2)}, u32[]{:S(2)}) %all-to-all-start.9) | async-done | bytes 1048608 | tf_op jit(solution)/shard_map/all_to_all | solution.py:21
  352.3 0.8 reshape.158
  (39 shorter events, 1.9 us)
Async XLA Ops:
  0.6 26.6 %copy-start = (bf16[1024,1024]{1,0:T(8,128)(2,1)S(1)}, bf16[1024,1024]{1,0:T(8,128)(2,1)}, u32[]{:S(2)}) copy-start(bf16[1024,1024]{1,0:T(8,128)(2,1)} %param.16) | copy-start | bytes 6291460
  2.6 11.7 %copy-start.8 = (s32[2048]{0:T(1024)S(1)}, s32[2048]{0:T(1024)}, u32[]{:S(2)}) copy-start(s32[2048]{0:T(1024)} %param.19) | copy-start | bytes 24580
  2.6 11.9 %copy-start.9 = (s32[128]{0:T(128)S(1)}, s32[128]{0:T(128)}, u32[]{:S(2)}) copy-start(s32[128]{0:T(128)} %param.18) | copy-start | bytes 1540
  6.6 8.0 %collective-permute-start.2 = (bf16[128,2048]{1,0:T(8,128)(2,1)S(1)}, bf16[128,2048]{1,0:T(8,128)(2,1)}, u32[]{:S(2)}, u32[]{:S(2)}) collective-permute-start(bf16[128,2048]{1,0:T(8,128)(2,1)S(1)} %slice.16), channel_id=1, source_target_pairs={{1,0},{2,1},{3,2},{4,3},{5,4},{6,5},{7,6},{8,7},{9,8},{10,9},{11,1... | collective-permute-start | bytes 1572872 | tf_op jit(solution)/shard_map/ppermute | solution.py:71
  7.9 6.7 %collective-permute-start.1 = (bf16[128,2048]{1,0:T(8,128)(2,1)S(1)}, bf16[128,2048]{1,0:T(8,128)(2,1)}, u32[]{:S(2)}, u32[]{:S(2)}) collective-permute-start(bf16[128,2048]{1,0:T(8,128)(2,1)S(1)} %slice.16), channel_id=1, source_target_pairs={{0,1},{1,2},{2,3},{3,4},{4,5},{5,6},{6,7},{7,8},{8,9},{9,10},{10,1... | collective-permute-start | bytes 1572872 | tf_op jit(solution)/shard_map/ppermute | solution.py:71
  15.9 4.5 %copy-start.7 = (bf16[128,1024]{0,1:T(8,128)(2,1)S(1)}, bf16[128,1024]{0,1:T(8,128)(2,1)}, u32[]{:S(2)}) copy-start(bf16[128,1024]{0,1:T(8,128)(2,1)} %copy.47) | copy-start | bytes 786436
  20.4 4.0 %copy-start.5 = (bf16[384,1024]{0,1:T(8,128)(2,1)S(1)}, bf16[384,1024]{0,1:T(8,128)(2,1)}, u32[]{:S(2)}) copy-start(bf16[384,1024]{0,1:T(8,128)(2,1)} %copy.46) | copy-start | bytes 2359300
  24.4 2.9 copy-start.3
  27.2 11.8 %copy-start.6 = (bf16[512,512]{1,0:T(8,128)(2,1)S(1)}, bf16[512,512]{1,0:T(8,128)(2,1)}, u32[]{:S(2)}) copy-start(bf16[512,512]{1,0:T(8,128)(2,1)} %param.11) | copy-start | bytes 1572868
  28.6 20.5 %all-to-all-start.6 = ((bf16[2,128,1024]{2,1,0:T(8,128)(2,1)}), bf16[2,128,1024]{2,1,0:T(8,128)(2,1)S(1)}, u32[]{:S(2)}, u32[]{:S(2)}) async-start(bf16[2,128,1024]{2,1,0:T(8,128)(2,1)} %broadcast_in_dim.38), calls=%async_computation.6 | async-start | bytes 1048576 | tf_op jit(solution)/shard_map/all_to_all | solution.py:21
  122.2 28.4 %all-to-all-start.7 = ((bf16[4,2,128,1024]{3,2,1,0:T(8,128)(2,1)}), bf16[4,2,128,1024]{3,2,1,0:T(8,128)(2,1)S(1)}, u32[]{:S(2)}, u32[]{:S(2)}) async-start(bf16[4,2,128,1024]{3,2,1,0:T(8,128)(2,1)} %broadcast_in_dim.39), calls=%async_computation.7 | async-start | bytes 4194304 | tf_op jit(solution)/shard_map/all_to_all | solution.py:21
  125.8 88.2 %collective-permute-start = (bf16[4,2,2,512,256]{4,3,2,1,0:T(8,128)(2,1)}, bf16[4,2,2,512,256]{4,3,2,1,0:T(8,128)(2,1)}, u32[]{:S(2)}, u32[]{:S(2)}) collective-permute-start(bf16[4,2,2,512,256]{4,3,2,1,0:T(8,128)(2,1)} %bitcast.57), channel_id=1, source_target_pairs={{0,1},{1,0},{2,3},{3,2},{4,5},{5,4},{6,7},{7,6},{8,9},{9,8},{10,11... | collective-permute-start | bytes 12582920 | tf_op jit(solution)/shard_map/ppermute | solution.py:134
  208.4 20.4 %all-to-all-start.8 = ((bf16[2,4,2,128,1024]{4,3,2,1,0:T(8,128)(2,1)}), bf16[2,4,2,128,1024]{4,3,2,1,0:T(8,128)(2,1)}, u32[]{:S(2)}, u32[]{:S(2)}) async-start(bf16[2,4,2,128,1024]{4,3,2,1,0:T(8,128)(2,1)} %broadcast_in_dim.40), calls=%async_computation.8 | async-start | bytes 8388608 | tf_op jit(solution)/shard_map/all_to_all | solution.py:21
  226.9 2.0 copy-start.2
  228.9 4.7 %copy-start.4 = (bf16[128,4096]{1,0:T(8,128)(2,1)S(1)}, bf16[128,4096]{1,0:T(8,128)(2,1)}, u32[]{:S(2)}) copy-start(bf16[128,4096]{1,0:T(8,128)(2,1)} %param.12) | copy-start | bytes 3145732
  228.9 54.4 %all-to-all-start.4 = ((bf16[8,1024,256]{2,1,0:T(8,128)(2,1)}), bf16[8,1024,256]{2,1,0:T(8,128)(2,1)}, u32[]{:S(2)}, u32[]{:S(2)}) async-start(bf16[8,1024,256]{2,1,0:T(8,128)(2,1)} %copy-done.2), calls=%async_computation.4 | async-start | bytes 8388608 | tf_op jit(solution)/shard_map/all_to_all | solution.py:21
  283.2 21.6 %all-to-all-start = ((bf16[16,128,256]{2,1,0:T(8,128)(2,1)}), bf16[16,128,256]{2,1,0:T(8,128)(2,1)S(1)}, u32[]{:S(2)}, u32[]{:S(2)}) async-start(bf16[16,128,256]{2,1,0:T(8,128)(2,1)} %bitcast.2), calls=%async_computation | async-start | bytes 2097152 | tf_op jit(solution)/shard_map/all_to_all | solution.py:21
  306.1 22.4 %all-to-all-start.5 = ((bf16[16,128,256]{2,1,0:T(8,128)(2,1)}), bf16[16,128,256]{2,1,0:T(8,128)(2,1)}, u32[]{:S(2)}, u32[]{:S(2)}) async-start(bf16[16,128,256]{2,1,0:T(8,128)(2,1)} %add_convert_fusion), calls=%async_computation.5 | async-start | bytes 2097152 | tf_op jit(solution)/shard_map/all_to_all | solution.py:21
  328.5 23.6 %all-to-all-start.9 = ((f32[128,8,256]{2,1,0:T(8,128)}), f32[128,8,256]{2,1,0:T(8,128)S(1)}, u32[]{:S(2)}, u32[]{:S(2)}) async-start(f32[128,8,256]{2,1,0:T(8,128)} %fusion.1), calls=%async_computation.9 | async-start | bytes 2097152 | tf_op jit(solution)/shard_map/all_to_all | solution.py:21
  333.1 19.9 %copy-start.1 = (bf16[1024,1024]{1,0:T(8,128)(2,1)S(1)}, bf16[1024,1024]{1,0:T(8,128)(2,1)}, u32[]{:S(2)}) copy-start(bf16[1024,1024]{1,0:T(8,128)(2,1)} %param.16) | copy-start | bytes 6291460
